TPU v7x, 32 devices: a whole 2x2x4 slice. The times are simulated.
32 devices in a mesh: inner: 8 (over z, y), cols: 4 (over x, core).
Axes of the slice: x: 2, y: 2, z: 4, core: 2. Of those that a mesh axis runs over, the one named last changes fastest.
Arguments:
- left_u: bfloat16 [64, 512, 128], P(('inner', 'cols')), may hold values from -6 to 6
- left_v: bfloat16 [64, 512, 128], P(('inner', 'cols')), may hold values from -0.0234375 to 0.0234375
- right_u: bfloat16 [16, 64, 512, 128], P('cols', 'inner'), may hold values from -6 to 6
- right_v: bfloat16 [16, 64, 512, 128], P('cols', 'inner'), may hold values from -0.1875 to 0.1875
- sketch: bfloat16 [16, 512, 128], P('cols'), may hold values from -0.25 to 0.25
- tile_index: int32 [16, 64], P('cols', 'inner'), may hold values from 0 to 63, as said below
- slot_mask: int32 [16, 64], P('cols', 'inner'), may hold values from 0 to 1, as said below
Outputs:
- basis: float32 [16, 512, 128], P('cols', 'inner')
- coeff: float32 [16, 512, 128], P('cols', 'inner')
Inputs may be any that keep to these rules, and one draw needn't show every extreme that they name: `tile_index`: slot s of an output tile belongs to inner group g = s // 8 and names a left tile of that group, g * 8 to g * 8 + 7; the tiles named by one output tile's slots of one group are distinct. `slot_mask`: in each output tile and inner group the live slots come first and there is at least one; in every output tile some group has all 8 slots live, and the others at most 4.
All inputs are finite; a program needn't handle non-finite values.
Results may differ from a plain program's by a relative error of at most 0.0045.
Values may be sent and summed in bfloat16 or wider, within the bound.
A program may use at most 64 MiB of HBM per device.

v0:
```python
import math
import jax
import jax.numpy as jnp
from jax import lax
from jax.sharding import PartitionSpec as P

NB = 512
HIGH = lax.Precision.HIGHEST


def orthonormal(sketch_rows, factor):
    solved = jax.scipy.linalg.solve_triangular(factor, jnp.swapaxes(sketch_rows, 1, 2), lower=True)
    return jnp.swapaxes(solved, 1, 2)


def gram_of(sketch_rows):
    return jnp.einsum("ona,onb->oab", sketch_rows, sketch_rows, precision=HIGH)


def body(left_u, left_v, right_u, right_v, sketch, tile_index, slot_mask):
    group_u, group_v = (
        lax.all_gather(left_u, "cols", axis=0, tiled=True),
        lax.all_gather(left_v, "cols", axis=0, tiled=True),
    )
    group_tiles = group_u.shape[0]
    local_idx = tile_index - lax.axis_index("inner") * group_tiles
    live_mask = slot_mask.astype(jnp.float32)[..., None, None]
    tile_u = jnp.take(group_u, local_idx, axis=0)
    tile_v = jnp.take(group_v, local_idx, axis=0)
    pairing = jnp.einsum("osna,osnb->osab", tile_v, right_u, preferred_element_type=jnp.float32)
    probes = jnp.einsum("osnb,ont->osbt", right_v, sketch, preferred_element_type=jnp.float32)
    mixing = (live_mask * jnp.einsum("osab,osbt->osat", pairing, probes, precision=HIGH)).astype(
        jnp.bfloat16
    )
    partial_sketch = jnp.einsum(
        "osna,osat->ont", tile_u, mixing, preferred_element_type=jnp.float32
    )
    scale_up = math.sqrt(NB)
    summed = lax.psum(partial_sketch, "inner")
    factor = jnp.linalg.cholesky(gram_of(summed))
    ortho = orthonormal(summed, factor)
    row_count = summed.shape[1] // lax.axis_size("inner")
    row_start = lax.axis_index("inner") * row_count
    basis = lax.dynamic_slice_in_dim(ortho, row_start, row_count, 1) * scale_up
    full_basis = ortho.astype(jnp.bfloat16)
    projected = jnp.einsum("osna,ont->osat", tile_u, full_basis, preferred_element_type=jnp.float32)
    backward = (
        live_mask * jnp.einsum("osab,osat->osbt", pairing, projected, precision=HIGH)
    ).astype(jnp.bfloat16)
    coeff_terms = jnp.einsum(
        "osnb,osbt->ont", right_v, backward, preferred_element_type=jnp.float32
    )
    coeff = lax.psum_scatter(coeff_terms, "inner", scatter_dimension=1, tiled=True)
    return (basis, coeff)


def solution(mesh):
    return jax.shard_map(
        body,
        mesh=mesh,
        in_specs=(
            P(("inner", "cols"), None, None),
            P(("inner", "cols"), None, None),
            P("cols", "inner", None, None),
            P("cols", "inner", None, None),
            P("cols", None, None),
            P("cols", "inner"),
            P("cols", "inner"),
        ),
        out_specs=(P("cols", "inner", None), P("cols", "inner", None)),
        check_vma=False,
    )
```

profile of v0, /device:TPU:0, one launch (start us, length us, event | category | flops | bytes accessed | tf_op | source)
XLA Modules:
  0.0 335.3 jit_solution(5929237776262730713)
XLA Ops:
  8.0 0.7 all-gather.3.cloned.1.call-update
  8.7 0.7 compare_and_fusion
  10.2 3.8 %fusion.10 = f32[4,8,128,128]{3,2,1,0:T(8,128)S(1)} fusion(bf16[4,8,512,128]{3,2,1,0:T(8,128)(2,1)} %param.12, bf16[4,512,128]{2,1,0:T(8,128)(2,1)S(1)} %copy-done), kind=kOutput, calls=%fused_computation.16 | convolution fusion | flops 536870912 | bytes 6815744 | tf_op jit(solution)/shard_map/osnb,ont->osbt/dot_general | solution.py:31
  14.0 15.0 %all-gather.5.cloned.1.call-done = bf16[8,512,128]{2,1,0:T(8,128)(2,1)} async-done(((bf16[2,512,128]{2,1,0:T(8,128)(2,1)}), bf16[8,512,128]{2,1,0:T(8,128)(2,1)}) %all-gather.5.cloned.1.call-update) | async-done | bytes 1048592 | tf_op jit(solution)/shard_map/all_gather | solution.py:23
  29.0 4.3 %gather_fusion.1 = bf16[32,512,128]{2,1,0:T(8,128)(2,1)} fusion(bf16[8,512,128]{2,1,0:T(8,128)(2,1)} %all-gather.5.cloned.1.call-done, s32[1024]{0:T(1024)S(1)} %pad_clamp_fusion), kind=kCustom, calls=%fused_computation.1.clone | custom fusion | bytes 8388736 | tf_op jit(solution)/shard_map/jit(_take)/gather | solution.py:29
  33.3 6.3 %copy.23 = bf16[4,8,512,128]{2,3,1,0:T(8,128)(2,1)} copy(bf16[4,8,512,128]{3,2,1,0:T(8,128)(2,1)} %bitcast.43) | data formatting | bytes 8388608 | tf_op jit(solution)/shard_map/jit(_take)/gather | solution.py:29
  39.6 7.7 %all-gather.3.cloned.1.call-done = bf16[8,512,128]{2,1,0:T(8,128)(2,1)} async-done(((bf16[2,512,128]{2,1,0:T(8,128)(2,1)}), bf16[8,512,128]{2,1,0:T(8,128)(2,1)}) %all-gather.3.cloned.1.call-update) | async-done | bytes 1048592 | tf_op jit(solution)/shard_map/all_gather | solution.py:22
  47.3 4.3 %gather_fusion = bf16[32,512,128]{2,1,0:T(8,128)(2,1)} fusion(bf16[8,512,128]{2,1,0:T(8,128)(2,1)} %all-gather.3.cloned.1.call-done, s32[1024]{0:T(1024)S(1)} %pad_clamp_fusion), kind=kCustom, calls=%fused_computation.clone | custom fusion | bytes 8388736 | tf_op jit(solution)/shard_map/jit(_take)/gather | solution.py:28
  51.6 6.2 %copy.22 = bf16[4,8,512,128]{2,3,1,0:T(8,128)(2,1)} copy(bf16[4,8,512,128]{3,2,1,0:T(8,128)(2,1)} %bitcast.42) | data formatting | bytes 8388608 | tf_op jit(solution)/shard_map/jit(_take)/gather | solution.py:28
  57.7 4.8 %fusion = f32[4,8,128,128]{3,2,1,0:T(8,128)S(1)} fusion(bf16[4,8,512,128]{3,2,1,0:T(8,128)(2,1)} %param.11, bf16[4,8,512,128]{2,3,1,0:T(8,128)(2,1)} %copy.23, pred[4,8]{1,0:T(4,128)(4,1)S(1)} %get-tuple-element.9), kind=kOutput, calls=%fused_computation.2 | convolution fusion | flops 538968064 | bytes 10485792 | tf_op jit(solution)/shard_map/osna,osnb->osab/dot_general | solution.py:30
  62.6 1.3 copy-done.3
  63.9 2.3 multiply_convert_fusion.1
  66.2 2.8 fusion.8
  69.3 78.1 %all-reduce.4.cloned.1.call-done = f32[4,512,128]{2,1,0:T(8,128)} async-done(((f32[4,512,128]{2,1,0:T(8,128)}), f32[4,512,128]{2,1,0:T(8,128)}) %all-reduce.4.cloned.1.call-update) | async-done | bytes 1048592 | tf_op jit(solution)/shard_map/psum | solution.py:39
  147.4 3.4 %fusion.19 = f32[4,128,128]{2,1,0:T(8,128)S(1)} fusion(f32[4,512,128]{2,1,0:T(8,128)} %all-reduce.4.cloned.1.call-done), kind=kOutput, calls=%fused_computation.36 | convolution fusion | flops 402653184 | bytes 1310720 | tf_op jit(solution)/shard_map/ona,onb->oab/dot_general | solution.py:17
  151.0 46.9 %custom-call.8 = f32[4,128,128]{2,1,0:T(8,128)S(1)} custom-call(f32[4,128,128]{2,1,0:T(8,128)S(1)} %fusion.15), custom_call_target="Cholesky" | custom-call | tf_op jit(solution)/shard_map/jit(cholesky)/cholesky | solution.py:40
  198.2 39.5 %custom-call.9 = f32[4,1,128,128]{2,3,1,0:T(8,128)S(1)} custom-call(f32[4,1,128,128]{3,2,1,0:T(8,128)S(1)} %select_bitcast_fusion), custom_call_target="InvertDiagBlocksLowerTriangular" | custom-call | tf_op jit(solution)/shard_map/jit(_solve_triangular)/vmap()/triangular_solve | solution.py:12
  237.7 1.0 fusion.13
  238.8 3.6 %fusion.3 = f32[4,8,128,128]{3,2,1,0:T(8,128)S(1)} fusion(bf16[4,8,512,128]{2,3,1,0:T(8,128)(2,1)} %copy.22, pred[4,8]{1,0:T(4,128)(4,1)S(1)} %get-tuple-element.9, f32[4,512,128]{2,1,0:T(8,128)S(1)} %fusion.13), kind=kOutput, calls=%fused_computation.6 | convolution fusion | flops 539230208 | bytes 7340064 | tf_op jit(solution)/shard_map/osna,ont->osat/dot_general | solution.py:46
  242.5 3.7 %multiply_convert_fusion = bf16[4,8,128,128]{3,2,1,0:T(8,128)(2,1)S(1)} fusion(f32[4,8,128,128]{3,2,1,0:T(8,128)S(1)} %copy-done.4, f32[4,8,128,128]{3,2,1,0:T(8,128)S(1)} %fusion.3, f32[4,8]{1,0:T(4,128)S(1)} %convert_element_type.12), kind=kOutput, calls=%fused_computation.11 | convolution fusion | flops 806354944 | bytes 5243008 | tf_op jit(solution)/shard_map/osab,osat->osbt/dot_general | solution.py:48
  246.2 1.5 convolution_bitcast_fusion
  247.7 1.4 copy.31
  251.1 76.1 %all-reduce.6.cloned.1.call-done = f32[4,512,128]{2,0,1:T(4,128)} async-done(((f32[4,512,128]{2,0,1:T(4,128)}), f32[4,512,128]{2,0,1:T(4,128)}) %all-reduce.6.cloned.1.call-update) | async-done | bytes 1048592
  327.2 0.9 constant_dynamic-slice_fusion
  (33 shorter events, 4.2 us)
Async XLA Ops:
  7.2 3.0 copy-start
  7.2 21.8 %all-gather.5.cloned.1.call-start = ((), (), s32[]{:S(2)}) async-start(), calls=%async_computation.1 | async-start | bytes 1310720 | tf_op jit(solution)/shard_map/all_gather | solution.py:23
  7.9 39.4 %all-gather.3.cloned.1.call-start = ((), (), s32[]{:S(2)}) async-start(), calls=%async_computation | async-start | bytes 1310720 | tf_op jit(solution)/shard_map/all_gather | solution.py:22
  8.7 138.7 %all-reduce.4.cloned.1.call-start = ((), (), s32[]{:S(2)}) async-start(), calls=%async_computation.2 | async-start | bytes 2097152 | tf_op jit(solution)/shard_map/psum | solution.py:39
  62.5 1.3 copy-start.3
  63.9 2.3 copy-start.5
  69.0 258.2 %all-reduce.6.cloned.1.call-start = ((), (), s32[]{:S(2)}) async-start(), calls=%async_computation.3 | async-start | bytes 2097152
  147.4 90.3 %copy-start.2 = (f32[4,512,128]{2,1,0:T(8,128)S(1)}, f32[4,512,128]{2,1,0:T(8,128)}, u32[]{:S(2)}) copy-start(f32[4,512,128]{2,1,0:T(8,128)} %all-reduce.4.cloned.1.call-done) | copy-start | bytes 3145732
  238.8 3.7 %copy-start.4 = (f32[4,8,128,128]{3,2,1,0:T(8,128)S(1)}, f32[4,8,128,128]{3,2,1,0:T(8,128)}, u32[]{:S(2)}) copy-start(f32[4,8,128,128]{3,2,1,0:T(8,128)} %copy-done.3) | copy-start | bytes 6291460
  242.4 3.8 %copy-start.1 = (bf16[4,8,512,128]{3,2,1,0:T(8,128)(2,1)S(1)}, bf16[4,8,512,128]{3,2,1,0:T(8,128)(2,1)}, u32[]{:S(2)}) copy-start(bf16[4,8,512,128]{3,2,1,0:T(8,128)(2,1)} %param.12) | copy-start | bytes 12582916
  246.2 2.9 copy-start.6
Sparse Core Ops, SparseCore 0:
  9.5 19.4 all-gather.4
  30.6 16.6 all-gather.2
  69.1 78.2 all-reduce.3
  249.3 77.8 all-reduce.5
where the time goes:
time: 336 us; the launch traced here: 335 us
  waiting for transfers between devices  178 us (53%)
  other arithmetic  88.8 us (26%)
  matrix products  27 us (8%)
  local copies, waits for them, and re-layouts  26.1 us (8%)
  between operations  14.6 us (4%)
    psum x1, waiting for transfers between devices, body(): summed = lax.psum(partial_sketch, 'inner')  78.1 us
    unnamed x5, waiting for transfers between devices  77.5 us
    another operation x4, other arithmetic, body(): factor = jnp.linalg.cholesky(gram_of(summed))  47.1 us
    another operation x3, other arithmetic, orthonormal(): jax.scipy.linalg.solve_triangular(factor, jnp.swapaxes(sketch_rows, 1, 2)...  39.7 us
    all_gather x1, waiting for transfers between devices, body(): lax.all_gather(left_v, 'cols', axis=0, tiled=True)  15 us
    gather x2, local copies, waits for them, and re-layouts, body(): tile_v = jnp.take(group_v, local_idx, axis=0)  10.6 us
    gather x2, local copies, waits for them, and re-layouts, body(): tile_u = jnp.take(group_u, local_idx, axis=0)  10.5 us
    all_gather x1, waiting for transfers between devices, body(): lax.all_gather(left_u, 'cols', axis=0, tiled=True)  7.72 us
  transfers between devices with their start and end apart: 4, of which 4 were waited for; matrix products, arithmetic and copies ran while one was open for 5% of the time, Pallas kernels for 0%

commit v1 on v0

--- a/solution.py
+++ b/solution.py
@@ -36,7 +36,8 @@
         "osna,osat->ont", tile_u, mixing, preferred_element_type=jnp.float32
     )
     scale_up = math.sqrt(NB)
-    summed = lax.psum(partial_sketch, "inner")
+    blocks = lax.all_gather(partial_sketch, "inner")
+    summed = jnp.sum(blocks, axis=0)
     factor = jnp.linalg.cholesky(gram_of(summed))
     ortho = orthonormal(summed, factor)
     row_count = summed.shape[1] // lax.axis_size("inner")

time: 336 us -> 383 us (1.14)
  waiting for transfers between devices: 178 us -> 223 us
  other arithmetic: 88.8 us -> 92.7 us
    all_gather x0 -> x1, waiting for transfers between devices: none -> 124 us  [body(): blocks = lax.all_gather(partial_sketch, 'inner')]
    psum x1 -> x0, waiting for transfers between devices: 78.1 us -> none  [body(): summed = lax.psum(partial_sketch, 'inner')]
    reduce_sum x0 -> x1, other arithmetic: none -> 3.91 us  [body(): summed = jnp.sum(blocks, axis=0)]
  transfers between devices with their start and end apart: 4 -> 4, of which waited for: 4 -> 4; matrix products, arithmetic and copies ran while one was open for 5% -> 4% of each run, Pallas kernels for 0% -> 0%
where the time goes in v1:
time: 383 us; the launch traced here: 382 us
  waiting for transfers between devices  223 us (58%)
  other arithmetic  92.7 us (24%)
  local copies, waits for them, and re-layouts  26.2 us (7%)
  matrix products  25.4 us (7%)
  between operations  14.6 us (4%)
    all_gather x1, waiting for transfers between devices, body(): blocks = lax.all_gather(partial_sketch, 'inner')  124 us
    unnamed x5, waiting for transfers between devices  76 us
    another operation x4, other arithmetic, body(): factor = jnp.linalg.cholesky(gram_of(summed))  47.1 us
    another operation x3, other arithmetic, orthonormal(): jax.scipy.linalg.solve_triangular(factor, jnp.swapaxes(sketch_rows, 1, 2)...  39.7 us
    all_gather x1, waiting for transfers between devices, body(): lax.all_gather(left_v, 'cols', axis=0, tiled=True)  15 us
    gather x2, local copies, waits for them, and re-layouts, body(): tile_v = jnp.take(group_v, local_idx, axis=0)  10.6 us
    gather x2, local copies, waits for them, and re-layouts, body(): tile_u = jnp.take(group_u, local_idx, axis=0)  10.5 us
    all_gather x1, waiting for transfers between devices, body(): lax.all_gather(left_u, 'cols', axis=0, tiled=True)  7.72 us
  transfers between devices with their start and end apart: 4, of which 4 were waited for; matrix products, arithmetic and copies ran while one was open for 4% of the time, Pallas kernels for 0%

profile of v1, /device:TPU:0, one launch (start us, length us, event | category | flops | bytes accessed | tf_op | source)
XLA Modules:
  0.0 382.4 jit_solution(5446981819117506402)
XLA Ops:
  8.0 0.7 all-gather.5.cloned.1.call-update
  10.2 3.8 fusion.10
  14.0 15.0 %all-gather.7.cloned.1.call-done = bf16[8,512,128]{2,1,0:T(8,128)(2,1)} async-done(((bf16[2,512,128]{2,1,0:T(8,128)(2,1)}), bf16[8,512,128]{2,1,0:T(8,128)(2,1)}) %all-gather.7.cloned.1.call-update) | async-done | bytes 1048592 | tf_op jit(solution)/shard_map/all_gather | solution.py:23
  29.0 4.3 %gather_fusion.1 = bf16[32,512,128]{2,1,0:T(8,128)(2,1)} fusion(bf16[8,512,128]{2,1,0:T(8,128)(2,1)} %all-gather.7.cloned.1.call-done, s32[1024]{0:T(1024)S(1)} %pad_clamp_fusion), kind=kCustom, calls=%fused_computation.1.clone | custom fusion | bytes 8388736 | tf_op jit(solution)/shard_map/jit(_take)/gather | solution.py:29
  33.3 6.3 %copy.23 = bf16[4,8,512,128]{2,3,1,0:T(8,128)(2,1)} copy(bf16[4,8,512,128]{3,2,1,0:T(8,128)(2,1)} %bitcast.44) | data formatting | bytes 8388608 | tf_op jit(solution)/shard_map/jit(_take)/gather | solution.py:29
  39.6 7.7 %all-gather.5.cloned.1.call-done = bf16[8,512,128]{2,1,0:T(8,128)(2,1)} async-done(((bf16[2,512,128]{2,1,0:T(8,128)(2,1)}), bf16[8,512,128]{2,1,0:T(8,128)(2,1)}) %all-gather.5.cloned.1.call-update) | async-done | bytes 1048592 | tf_op jit(solution)/shard_map/all_gather | solution.py:22
  47.3 4.3 %gather_fusion = bf16[32,512,128]{2,1,0:T(8,128)(2,1)} fusion(bf16[8,512,128]{2,1,0:T(8,128)(2,1)} %all-gather.5.cloned.1.call-done, s32[1024]{0:T(1024)S(1)} %pad_clamp_fusion), kind=kCustom, calls=%fused_computation.clone | custom fusion | bytes 8388736 | tf_op jit(solution)/shard_map/jit(_take)/gather | solution.py:28
  51.6 6.2 %copy.22 = bf16[4,8,512,128]{2,3,1,0:T(8,128)(2,1)} copy(bf16[4,8,512,128]{3,2,1,0:T(8,128)(2,1)} %bitcast.43) | data formatting | bytes 8388608 | tf_op jit(solution)/shard_map/jit(_take)/gather | solution.py:28
  57.8 4.8 %fusion = f32[4,8,128,128]{3,2,1,0:T(8,128)S(1)} fusion(bf16[4,8,512,128]{3,2,1,0:T(8,128)(2,1)} %param.11, bf16[4,8,512,128]{2,3,1,0:T(8,128)(2,1)} %copy.23, pred[4,8]{1,0:T(4,128)(4,1)S(1)} %get-tuple-element.9), kind=kOutput, calls=%fused_computation.2 | convolution fusion | flops 538968064 | bytes 10485792 | tf_op jit(solution)/shard_map/osna,osnb->osab/dot_general | solution.py:30
  62.6 1.3 copy-done.2
  63.9 2.3 multiply_convert_fusion.1
  66.2 2.8 fusion.8
  69.3 124.4 %all-gather.9.cloned.1.call-done = f32[32,512,128]{2,1,0:T(8,128)} async-done(((f32[4,512,128]{2,1,0:T(8,128)}), f32[32,512,128]{2,1,0:T(8,128)}) %all-gather.9.cloned.1.call-update) | async-done | bytes 8388624 | tf_op jit(solution)/shard_map/all_gather | solution.py:39
  193.7 3.9 %reduce_sum.9 = f32[4,512,128]{2,1,0:T(8,128)S(1)} reduce(f32[8,4,512,128]{3,2,1,0:T(8,128)} %bitcast.45, f32[]{:T(128)} %constant.64.clone.1), dimensions={0}, to_apply=%region_0.0 | reduce | flops 1835008 | bytes 9437188 | tf_op jit(solution)/shard_map/reduce_sum | solution.py:40
  197.6 1.8 fusion.19
  199.6 46.9 %custom-call.8 = f32[4,128,128]{2,1,0:T(8,128)S(1)} custom-call(f32[4,128,128]{2,1,0:T(8,128)S(1)} %fusion.15), custom_call_target="Cholesky" | custom-call | tf_op jit(solution)/shard_map/jit(cholesky)/cholesky | solution.py:41
  246.8 39.5 %custom-call.9 = f32[4,1,128,128]{2,3,1,0:T(8,128)S(1)} custom-call(f32[4,1,128,128]{3,2,1,0:T(8,128)S(1)} %select_bitcast_fusion), custom_call_target="InvertDiagBlocksLowerTriangular" | custom-call | tf_op jit(solution)/shard_map/jit(_solve_triangular)/vmap()/triangular_solve | solution.py:12
  286.3 1.0 fusion.13
  287.4 3.6 fusion.3
  291.0 3.7 multiply_convert_fusion
  294.8 1.5 convolution_bitcast_fusion
  296.3 1.4 copy.31
  299.7 74.6 %all-reduce.3.cloned.1.call-done = f32[4,512,128]{2,0,1:T(4,128)} async-done(((f32[4,512,128]{2,0,1:T(4,128)}), f32[4,512,128]{2,0,1:T(4,128)}) %all-reduce.3.cloned.1.call-update) | async-done | bytes 1048592
  374.3 0.9 constant_dynamic-slice_fusion
  (32 shorter events, 4.9 us)
Async XLA Ops:
  7.2 3.0 copy-start
  7.2 21.8 %all-gather.7.cloned.1.call-start = ((), (), s32[]{:S(2)}) async-start(), calls=%async_computation.1 | async-start | bytes 1310720 | tf_op jit(solution)/shard_map/all_gather | solution.py:23
  7.9 39.4 %all-gather.5.cloned.1.call-start = ((), (), s32[]{:S(2)}) async-start(), calls=%async_computation | async-start | bytes 1310720 | tf_op jit(solution)/shard_map/all_gather | solution.py:22
  8.7 185.0 %all-gather.9.cloned.1.call-start = ((), (), s32[]{:S(2)}) async-start(), calls=%async_computation.2 | async-start | bytes 9437184 | tf_op jit(solution)/shard_map/all_gather | solution.py:39
  62.6 1.3 copy-start.2
  63.9 2.3 copy-start.4
  69.1 305.2 %all-reduce.3.cloned.1.call-start = ((), (), s32[]{:S(2)}) async-start(), calls=%async_computation.3 | async-start | bytes 2097152
  287.4 3.7 copy-start.3
  291.0 3.8 copy-start.1
  294.8 2.9 copy-start.5
Sparse Core Ops, SparseCore 0:
  9.5 19.4 all-gather.6
  30.6 16.6 all-gather.4
  69.2 124.4 all-gather.8
  297.8 76.3 all-reduce.2
